TPU v7x, 128 devices: a whole 4x4x4 slice. The times are simulated.
128 devices in a mesh: store: 8 (over z_lo, y), mod: 16 (over z_hi, x, core).
Axes of the slice: x: 4, y: 4, z: 4 (z_hi: 2, z_lo: 2; z = z_hi * 2 + z_lo), core: 2. Of those that a mesh axis runs over, the one named last changes fastest.
Arguments:
- act_proj: bfloat16 [1024, 256, 1024], P(('store', 'mod')), may hold values from -1.5 to 1.5
- grad_proj: bfloat16 [1024, 256, 1024], P(('store', 'mod')), may hold values from -1.5 to 1.5
- token_mask: int32 [1024, 256], P(('store', 'mod')), may hold values 0 or 1
- layer_of: int32 [32], P('mod'), may hold values from 0 to 3, as said below
- layer_weight: float32 [4], replicated, may hold values from 0.25 to 4
- fisher_inv: bfloat16 [32, 1024, 1024], P('mod'), may hold values from -0.2 to 1.8
- stored_grads: bfloat16 [32768, 32768], P('store', 'mod'), may hold values from -0.049804688 to 0.049804688
Outputs:
- scores: float32 [1024, 32768], P('mod', 'store')
Inputs may be any that keep to these rules, and one draw needn't show every extreme that they name: `layer_of`: each of the 4 layers holds the same number of modules.
All inputs are finite; a program needn't handle non-finite values. No bound on the sum of `token_mask` on one device may be relied on, other than what follows from the above.
Results may differ from a plain program's by a relative error of at most 0.004.
Values may be sent and summed in bfloat16 or wider, within the bound.
No kernel may reach another device: no remote copies, remote signals or barrier semaphores. Data moves between devices by JAX's collectives and lax.ppermute only.
A program may use at most 128 MiB of HBM per device.

v0:
```python
import jax
import jax.numpy as jnp
from jax import lax
from jax.sharding import PartitionSpec as P

R = 32


def local(act_proj, grad_proj, token_mask, layer_of, layer_weight, fisher_inv, stored_grads):
    q_local, length, columns = act_proj.shape
    modules = columns // R
    valid_mask = token_mask.astype(jnp.bfloat16)[:, :, None]
    grad_side = (grad_proj * valid_mask).reshape(q_local, length, modules, R)
    act_side = act_proj.reshape(q_local, length, modules, R)
    per_sample = jnp.einsum(
        "qtmi,qtmj->qmij", grad_side, act_side, preferred_element_type=jnp.float32
    )
    per_sample = per_sample.reshape(q_local, modules, R * R).astype(jnp.bfloat16)
    picked = layer_of[:, None] == jnp.arange(layer_weight.shape[0], dtype=jnp.int32)[None, :]
    module_weight = jnp.sum(jnp.where(picked, layer_weight[None, :], 0.0), axis=1)
    grouped = lax.all_to_all(per_sample, "mod", split_axis=1, concat_axis=0, tiled=True)
    product = jnp.einsum("qkr,krc->qkc", grouped, fisher_inv, preferred_element_type=jnp.float32)
    conditioned = (product * module_weight[None, :, None]).astype(jnp.bfloat16)
    everyone = lax.all_gather(conditioned, "store", axis=0, tiled=True)
    flat_rows = everyone.reshape(everyone.shape[0], -1)
    return lax.psum_scatter(
        lax.dot_general(
            flat_rows, stored_grads, (((1,), (1,)), ((), ())), preferred_element_type=jnp.float32
        ),
        "mod",
        scatter_dimension=0,
        tiled=True,
    )


def solution(mesh):
    in_specs = (
        P(("store", "mod"), None, None),
        P(("store", "mod"), None, None),
        P(("store", "mod"), None),
        P("mod"),
        P(),
        P("mod", None, None),
        P("store", "mod"),
    )
    out_specs = P("mod", "store")
    return jax.shard_map(local, mesh=mesh, in_specs=in_specs, out_specs=out_specs, check_vma=False)
```

profile of v0, /device:TPU:0, one launch (start us, length us, event | category | flops | bytes accessed | tf_op | source)
XLA Modules:
  0.0 285.2 jit_solution(10545839637817417900)
XLA Ops:
  6.5 0.7 convert_element_type.15
  7.2 6.4 %copy.21 = bf16[8,256,1024]{1,2,0:T(8,128)(2,1)} copy(bf16[8,256,1024]{2,1,0:T(8,128)(2,1)} %param.7) | data formatting | bytes 8388608 | tf_op args[0]
  13.7 6.5 %copy.20 = bf16[8,256,1024]{1,2,0:T(8,128)(2,1)} copy(bf16[8,256,1024]{2,1,0:T(8,128)(2,1)} %param.8) | data formatting | bytes 8388608 | tf_op args[1]
  20.2 2.6 broadcast_multiply_fusion
  22.8 0.8 copy-done
  23.6 1.2 convolution_convert_fusion
  24.9 0.0 copy-start.1
  24.9 0.0 copy-start.2
  24.9 2.2 convert_element_type.17
  27.1 1.1 copy.22
  28.2 7.8 %all-to-all-start = ((bf16[8,32,1024]{2,0,1:T(8,128)(2,1)}), bf16[8,32,1024]{2,0,1:T(8,128)(2,1)S(1)}, u32[]{:S(2)}, u32[]{:S(2)}) async-start(bf16[8,32,1024]{2,0,1:T(8,128)(2,1)} %copy.22), calls=%async_computation | async-start | bytes 1048576 | tf_op jit(solution)/shard_map/all_to_all | solution.py:21
  36.0 0.0 all-gather.2.cloned.1.call-start
  36.1 0.0 copy-done.1
  36.1 0.0 copy-done.2
  36.1 0.2 fusion.4
  36.3 12.1 %all-to-all-done = bf16[8,32,1024]{2,0,1:T(8,128)(2,1)S(1)} async-done(((bf16[8,32,1024]{2,0,1:T(8,128)(2,1)}), bf16[8,32,1024]{2,0,1:T(8,128)(2,1)S(1)}, u32[]{:S(2)}, u32[]{:S(2)}) %all-to-all-start) | async-done | bytes 524320 | tf_op jit(solution)/shard_map/all_to_all | solution.py:21
  48.4 3.7 %fusion.1 = bf16[128,2,1024]{2,0,1:T(8,128)(2,1)} fusion(bf16[2,1024,1024]{2,1,0:T(8,128)(2,1)} %param.12, bf16[8,16,2,1024]{3,0,2,1:T(8,128)(2,1)S(1)} %bitcast.21, f32[2]{0:T(128)S(1)} %fusion.4), kind=kOutput, calls=%fused_computation.4 | convolution fusion | flops 537395200 | bytes 5242888 | tf_op jit(solution)/shard_map/qkr,krc->qkc/dot_general | solution.py:22
  52.1 0.0 all-gather.2.cloned.1.call-update
  52.1 0.0 reduce-scatter.2.cloned.1.call-start
  52.2 49.7 %all-gather.2.cloned.1.call-done = bf16[1024,2,1024]{2,0,1:T(8,128)(2,1)} async-done(((bf16[128,2,1024]{2,0,1:T(8,128)(2,1)}), bf16[1024,2,1024]{2,0,1:T(8,128)(2,1)}) %all-gather.2.cloned.1.call-update) | async-done | bytes 4194320 | tf_op jit(solution)/shard_map/all_gather | solution.py:24
  101.9 6.2 %copy.24 = bf16[1024,2,1024]{0,2,1:T(8,128)(2,1)} copy(bf16[1024,2,1024]{2,0,1:T(8,128)(2,1)} %all-gather.2.cloned.1.call-done) | data formatting | bytes 8388608 | tf_op jit(solution)/shard_map/all_gather | solution.py:24
  108.1 23.6 %fusion.5 = f32[1024,4096]{1,0:T(8,128)} fusion(bf16[1024,2048]{0,1:T(8,128)(2,1)} %bitcast.20, bf16[4096,2048]{1,0:T(8,128)(2,1)} %param.13), kind=kOutput, calls=%fused_computation.9 | convolution fusion | flops 17179869184 | bytes 37748736 | tf_op jit(solution)/shard_map/dot_general | solution.py:27
  131.7 0.0 reduce-scatter.2.cloned.1.call-update
  131.7 146.6 %reduce-scatter.2.cloned.1.call-done = f32[64,4096]{1,0:T(8,128)} async-done(((f32[1024,4096]{1,0:T(8,128)}), f32[64,4096]{1,0:T(8,128)}) %reduce-scatter.2.cloned.1.call-update) | async-done | bytes 1048592 | tf_op jit(solution)/shard_map/reduce_scatter | solution.py:26
  (1 shorter events, 0.0 us)
Async XLA Ops:
  20.2 3.4 %copy-start = (bf16[8,256,1024]{1,2,0:T(8,128)(2,1)S(1)}, bf16[8,256,1024]{1,2,0:T(8,128)(2,1)}, u32[]{:S(2)}) copy-start(bf16[8,256,1024]{1,2,0:T(8,128)(2,1)} %copy.21) | copy-start | bytes 12582916
  24.9 11.2 %copy-start.1 = (f32[4]{0:T(128)S(1)}, f32[4]{0:T(128)}, u32[]{:S(2)}) copy-start(f32[4]{0:T(128)} %param.11) | copy-start | bytes 52
  24.9 11.2 %copy-start.2 = (s32[2]{0:T(128)S(1)}, s32[2]{0:T(128)}, u32[]{:S(2)}) copy-start(s32[2]{0:T(128)} %param.10) | copy-start | bytes 28
  28.2 20.2 %all-to-all-start = ((bf16[8,32,1024]{2,0,1:T(8,128)(2,1)}), bf16[8,32,1024]{2,0,1:T(8,128)(2,1)S(1)}, u32[]{:S(2)}, u32[]{:S(2)}) async-start(bf16[8,32,1024]{2,0,1:T(8,128)(2,1)} %copy.22), calls=%async_computation | async-start | bytes 1048576 | tf_op jit(solution)/shard_map/all_to_all | solution.py:21
  36.0 65.8 %all-gather.2.cloned.1.call-start = ((), (), s32[]{:S(2)}) async-start(), calls=%async_computation.2 | async-start | bytes 4718592 | tf_op jit(solution)/shard_map/all_gather | solution.py:24
  52.1 226.2 %reduce-scatter.2.cloned.1.call-start = ((), (), s32[]{:S(2)}) async-start(), calls=%async_computation.3 | async-start | bytes 17825792 | tf_op jit(solution)/shard_map/reduce_scatter | solution.py:26
Sparse Core Ops, SparseCore 0:
  52.2 49.5 all-gather.1
  131.8 146.4 reduce-scatter.1
where the time goes:
time: 286 us; the launch traced here: 285 us
  waiting for transfers between devices  208 us (73%)
  matrix products  28.5 us (10%)
  local copies, waits for them, and re-layouts  23.3 us (8%)
  between operations  13.5 us (5%)
  starting transfers between devices  7.91 us (3%)
  other arithmetic  3.49 us (1%)
    reduce_scatter x1, waiting for transfers between devices, local(): lax.psum_scatter(lax.dot_general(flat_rows, stored_grads, (((1,), (1,)),...  147 us
    all_gather x1, waiting for transfers between devices, local(): everyone = lax.all_gather(conditioned, 'store', axis=0, tiled=True)  49.7 us
    dot_general x1, matrix products, local(): lax.dot_general(flat_rows, stored_grads, (((1,), (1,)), ((), ())), prefer...  23.6 us
    unnamed x8, local copies, waits for them, and re-layouts  13.8 us
    all_to_all x1, waiting for transfers between devices, local(): lax.all_to_all(per_sample, 'mod', split_axis=1, concat_axis=0, tiled=True)  12.1 us
    all_to_all x1, starting transfers between devices, local(): lax.all_to_all(per_sample, 'mod', split_axis=1, concat_axis=0, tiled=True)  7.83 us
    all_gather x1, local copies, waits for them, and re-layouts, local(): everyone = lax.all_gather(conditioned, 'store', axis=0, tiled=True)  6.22 us
  transfers between devices with their start and end apart: 3, of which 3 were waited for; matrix products, arithmetic and copies ran while one was open for 0% of the time, Pallas kernels for 0%

commit v1 on v0

--- a/solution.py
+++ b/solution.py
@@ -18,7 +18,10 @@
     per_sample = per_sample.reshape(q_local, modules, R * R).astype(jnp.bfloat16)
     picked = layer_of[:, None] == jnp.arange(layer_weight.shape[0], dtype=jnp.int32)[None, :]
     module_weight = jnp.sum(jnp.where(picked, layer_weight[None, :], 0.0), axis=1)
-    grouped = lax.all_to_all(per_sample, "mod", split_axis=1, concat_axis=0, tiled=True)
+    grouped = jnp.concatenate(
+        lax.all_to_all(jnp.stack(jnp.split(per_sample, lax.axis_size("mod"), axis=1)), "mod", 0, 0),
+        axis=0,
+    )
     product = jnp.einsum("qkr,krc->qkc", grouped, fisher_inv, preferred_element_type=jnp.float32)
     conditioned = (product * module_weight[None, :, None]).astype(jnp.bfloat16)
     everyone = lax.all_gather(conditioned, "store", axis=0, tiled=True)

time: 286 us -> 295 us (1.031)
  local copies, waits for them, and re-layouts: 23.3 us -> 32.6 us
    unnamed x8 -> x23, local copies, waits for them, and re-layouts: 13.8 us -> 23.5 us
where the time goes in v1:
time: 295 us; the launch traced here: 294 us
  waiting for transfers between devices  208 us (71%)
  local copies, waits for them, and re-layouts  32.6 us (11%)
  matrix products  28.6 us (10%)
  between operations  13.5 us (5%)
  starting transfers between devices  7.91 us (3%)
  other arithmetic  3.49 us (1%)
    reduce_scatter x1, waiting for transfers between devices, local(): lax.psum_scatter(lax.dot_general(flat_rows, stored_grads, (((1,), (1,)),...  147 us
    all_gather x1, waiting for transfers between devices, local(): everyone = lax.all_gather(conditioned, 'store', axis=0, tiled=True)  49.7 us
    dot_general x1, matrix products, local(): lax.dot_general(flat_rows, stored_grads, (((1,), (1,)), ((), ())), prefer...  23.6 us
    unnamed x23, local copies, waits for them, and re-layouts  23.5 us
    all_to_all x1, waiting for transfers between devices, local(): lax.all_to_all(jnp.stack(jnp.split(per_sample, lax.axis_size('mod'), axis...  12.1 us
    all_to_all x1, starting transfers between devices, local(): lax.all_to_all(jnp.stack(jnp.split(per_sample, lax.axis_size('mod'), axis...  7.83 us
    all_gather x1, local copies, waits for them, and re-layouts, local(): everyone = lax.all_gather(conditioned, 'store', axis=0, tiled=True)  6.22 us
  transfers between devices with their start and end apart: 3, of which 3 were waited for; matrix products, arithmetic and copies ran while one was open for 0% of the time, Pallas kernels for 0%

profile of v1, /device:TPU:0, one launch (start us, length us, event | category | flops | bytes accessed | tf_op | source)
XLA Modules:
  0.0 294.5 jit_solution(13858655958997649589)
XLA Ops:
  6.5 0.7 convert_element_type.15
  7.2 6.4 %copy.16 = bf16[8,256,1024]{1,2,0:T(8,128)(2,1)} copy(bf16[8,256,1024]{2,1,0:T(8,128)(2,1)} %param.7) | data formatting | bytes 8388608 | tf_op args[0]
  13.7 6.5 %copy.15 = bf16[8,256,1024]{1,2,0:T(8,128)(2,1)} copy(bf16[8,256,1024]{2,1,0:T(8,128)(2,1)} %param.8) | data formatting | bytes 8388608 | tf_op args[1]
  20.2 2.6 broadcast_multiply_fusion
  22.8 0.8 copy-done
  23.6 1.2 convolution_convert_fusion
  24.9 2.2 convert_element_type.17
  27.8 0.7 constant_dynamic-update-slice_fusion.14
  28.4 0.7 constant_dynamic-update-slice_fusion.13
  29.1 0.7 constant_dynamic-update-slice_fusion.12
  30.4 0.7 constant_dynamic-update-slice_fusion.10
  31.0 0.7 constant_dynamic-update-slice_fusion.9
  33.6 0.7 constant_dynamic-update-slice_fusion.5
  34.2 0.7 constant_dynamic-update-slice_fusion.4
  35.5 0.7 constant_dynamic-update-slice_fusion.2
  36.2 0.7 constant_dynamic-update-slice_fusion.1
  36.8 0.7 constant_dynamic-update-slice_fusion
  37.5 7.8 %all-to-all-start = ((bf16[16,8,2,1024]{3,2,1,0:T(2,128)(2,1)}), bf16[16,8,2,1024]{3,2,1,0:T(2,128)(2,1)S(1)}, u32[]{:S(2)}, u32[]{:S(2)}) async-start(bf16[16,8,2,1024]{3,2,1,0:T(2,128)(2,1)} %constant_dynamic-update-slice_fusion), calls=%async_computation | async-start | bytes 1048576 | tf_op jit(solution)/shard_map/all_to_all | solution.py:22
  45.6 12.1 %all-to-all-done = bf16[16,8,2,1024]{3,2,1,0:T(2,128)(2,1)S(1)} async-done(((bf16[16,8,2,1024]{3,2,1,0:T(2,128)(2,1)}), bf16[16,8,2,1024]{3,2,1,0:T(2,128)(2,1)S(1)}, u32[]{:S(2)}, u32[]{:S(2)}) %all-to-all-start) | async-done | bytes 524320 | tf_op jit(solution)/shard_map/all_to_all | solution.py:22
  57.7 3.8 %fusion.1 = bf16[128,2,1024]{2,0,1:T(8,128)(2,1)} fusion(bf16[2,1024,1024]{2,1,0:T(8,128)(2,1)} %param.12, bf16[16,8,2,1024]{3,2,1,0:T(2,128)(2,1)S(1)} %all-to-all-done, f32[2]{0:T(128)S(1)} %fusion.4), kind=kOutput, calls=%fused_computation.4 | convolution fusion | flops 537395200 | bytes 5242888 | tf_op jit(solution)/shard_map/qkr,krc->qkc/dot_general | solution.py:25
  61.5 49.7 %all-gather.2.cloned.1.call-done = bf16[1024,2,1024]{2,0,1:T(8,128)(2,1)} async-done(((bf16[128,2,1024]{2,0,1:T(8,128)(2,1)}), bf16[1024,2,1024]{2,0,1:T(8,128)(2,1)}) %all-gather.2.cloned.1.call-update) | async-done | bytes 4194320 | tf_op jit(solution)/shard_map/all_gather | solution.py:27
  111.2 6.2 %copy.18 = bf16[1024,2,1024]{0,2,1:T(8,128)(2,1)} copy(bf16[1024,2,1024]{2,0,1:T(8,128)(2,1)} %all-gather.2.cloned.1.call-done) | data formatting | bytes 8388608 | tf_op jit(solution)/shard_map/all_gather | solution.py:27
  117.4 23.6 %fusion.5 = f32[1024,4096]{1,0:T(8,128)} fusion(bf16[1024,2048]{0,1:T(8,128)(2,1)} %bitcast.81, bf16[4096,2048]{1,0:T(8,128)(2,1)} %param.13), kind=kOutput, calls=%fused_computation.41 | convolution fusion | flops 17179869184 | bytes 37748736 | tf_op jit(solution)/shard_map/dot_general | solution.py:30
  141.0 146.6 %reduce-scatter.2.cloned.1.call-done = f32[64,4096]{1,0:T(8,128)} async-done(((f32[1024,4096]{1,0:T(8,128)}), f32[64,4096]{1,0:T(8,128)}) %reduce-scatter.2.cloned.1.call-update) | async-done | bytes 1048592 | tf_op jit(solution)/shard_map/reduce_scatter | solution.py:29
  (16 shorter events, 4.2 us)
Async XLA Ops:
  20.2 3.4 %copy-start = (bf16[8,256,1024]{1,2,0:T(8,128)(2,1)S(1)}, bf16[8,256,1024]{1,2,0:T(8,128)(2,1)}, u32[]{:S(2)}) copy-start(bf16[8,256,1024]{1,2,0:T(8,128)(2,1)} %copy.16) | copy-start | bytes 12582916
  24.9 20.5 %copy-start.1 = (f32[4]{0:T(128)S(1)}, f32[4]{0:T(128)}, u32[]{:S(2)}) copy-start(f32[4]{0:T(128)} %param.11) | copy-start | bytes 52
  24.9 20.5 %copy-start.2 = (s32[2]{0:T(128)S(1)}, s32[2]{0:T(128)}, u32[]{:S(2)}) copy-start(s32[2]{0:T(128)} %param.10) | copy-start | bytes 28
  37.5 20.2 %all-to-all-start = ((bf16[16,8,2,1024]{3,2,1,0:T(2,128)(2,1)}), bf16[16,8,2,1024]{3,2,1,0:T(2,128)(2,1)S(1)}, u32[]{:S(2)}, u32[]{:S(2)}) async-start(bf16[16,8,2,1024]{3,2,1,0:T(2,128)(2,1)} %constant_dynamic-update-slice_fusion), calls=%async_computation | async-start | bytes 1048576 | tf_op jit(solution)/shard_map/all_to_all | solution.py:22
  45.3 65.9 %all-gather.2.cloned.1.call-start = ((), (), s32[]{:S(2)}) async-start(), calls=%async_computation.2 | async-start | bytes 4718592 | tf_op jit(solution)/shard_map/all_gather | solution.py:27
  61.4 226.2 %reduce-scatter.2.cloned.1.call-start = ((), (), s32[]{:S(2)}) async-start(), calls=%async_computation.3 | async-start | bytes 17825792 | tf_op jit(solution)/shard_map/reduce_scatter | solution.py:29
Sparse Core Ops, SparseCore 0:
  61.5 49.5 all-gather.1
  141.1 146.4 reduce-scatter.1
